TPU v7x, 128 devices: a whole 4x4x4 slice. The times are simulated.
128 devices in a mesh: gx: 16 (over z, y), gy: 8 (over x, core).
Axes of the slice: x: 4, y: 4, z: 4, core: 2. Of those that a mesh axis runs over, the one named last changes fastest.
Arguments:
- jacobian: bfloat16 [16384, 192, 384], P(('gx', 'gy')), may hold values from -0.3125 to 0.3125
- grain_slots: int32 [16384, 64], P(('gx', 'gy')), may hold values from 0 to 18431, as said below
- block_count: int32 [128], P(('gx', 'gy')), may hold values from 1 to 128, as said below
- impulse_start: float32 [16384, 192], P(('gx', 'gy')), may hold values from -3 to 3
- velocity_bias: float32 [16384, 192], P(('gx', 'gy')), may hold values from -6 to 6
- friction: float32 [16384, 64], P(('gx', 'gy')), may hold values from 0.2 to 0.8
- free_velocity: float32 [6, 262144], P(None, ('gx', 'gy')), may hold values from -6 to 6
- inverse_mass: float32 [6, 262144], P(None, ('gx', 'gy')), may hold values from 0.5 to 4
Outputs:
- impulses: float32 [16384, 192], P(('gx', 'gy'))
- velocities: float32 [6, 262144], P(None, ('gx', 'gy'))
Inputs may be any that keep to these rules, and one draw needn't show every extreme that they name: `grain_slots`: A slot value s * 2048 + l names grain l of the device at offset (s // 3 - 1, s % 3 - 1) along (gx, gy) from the block's device (the device holding the block's row); that device always exists. A device's first block_count block slots are live, the rest are not; some device has all 128 live.
All inputs are finite; a program needn't handle non-finite values.
Results may differ from a plain program's by a relative error of at most 0.014.
Values may be sent and summed in bfloat16 or wider, within the bound.
A program may use at most 128 MiB of HBM per device.

v0:
```python
import math
import jax
import jax.numpy as jnp
from jax import lax
from jax.sharding import Mesh
from jax.sharding import PartitionSpec as P

CB = 64
GB = 64
ITERS = 3
GX_GY = ("gx_0", "gx_1", "gy_0", "gy_1")
GX = ("gx_0", "gx_1")
GY = ("gy_0", "gy_1")
epsilon = 1e-06


def with_halo(array, sides, width):
    for axis, dim in sides:
        size, length = (lax.axis_size(axis), array.shape[dim])
        up = [(i, (i + 1) % size) for i in range(size - 1)]
        down = [(j, i) for i, j in up]
        last = lax.slice_in_dim(array, length - width, length, axis=dim)
        leading = lax.slice_in_dim(array, 0, width, axis=dim)
        before = lax.ppermute(last, axis, up)
        after = lax.ppermute(leading, axis, down)
        array = jnp.concatenate([before, array, after], axis=dim)
    return array


def from_behind(block, axis, distance):
    devices = range(lax.axis_size(axis))
    route = [(i - distance, i) for i in devices if i - distance in devices]
    return lax.ppermute(block, axis, route)


def one_axis_at_a_time(array, axes):
    for axis in axes:
        array = lax.psum(array, axis)
    return array


def momentum_weights(iterations):
    momentum = 1.0
    weights = []
    for iteration in range(iterations):
        upcoming = (-momentum * momentum + momentum * math.sqrt(momentum * momentum + 4.0)) / 2.0
        weights.append(momentum * (1.0 - momentum) / (momentum * momentum + upcoming))
        momentum = upcoming
    return weights


def project_cone(target, friction):
    normal = target[:, :CB]
    tangent_one = target[:, CB : 2 * CB]
    tangent_two = target[:, 2 * CB :]
    tangent_norm = jnp.sqrt(tangent_one * tangent_one + tangent_two * tangent_two)
    inside = tangent_norm <= friction * normal
    opposite = friction * tangent_norm <= -normal
    cone_normal = (normal + friction * tangent_norm) / (1.0 + friction * friction)
    cone_ratio = friction * cone_normal / jnp.where(tangent_norm > 0, tangent_norm, 1.0)
    new_normal = jnp.where(inside, normal, jnp.where(opposite, 0.0, cone_normal))
    shrink = jnp.where(inside, 1.0, jnp.where(opposite, 0.0, cone_ratio))
    return jnp.concatenate([new_normal, tangent_one * shrink, tangent_two * shrink], axis=1)


def shards(
    jacobian,
    grain_slots,
    block_count,
    impulse_start,
    velocity_bias,
    friction,
    free_velocity,
    inverse_mass,
):
    blocks = jacobian.shape[0]
    grains = free_velocity.shape[1]
    live_mask = (jnp.arange(blocks, dtype=jnp.int32) < block_count[0]).astype(jnp.float32)[:, None]

    def forward(grain_field):
        nearby = with_halo(grain_field.reshape(6, 1, 1, grains), ((GX, 1), (GY, 2)), 1)
        nearby = nearby.reshape(6, 9 * grains)
        picked = jnp.take(nearby, grain_slots, axis=1)
        picked = jnp.transpose(picked, (1, 0, 2)).reshape(blocks, 6 * GB)
        return jnp.einsum("bij,bj->bi", jacobian, picked, preferred_element_type=jnp.float32)

    def backward(impulse_field):
        pushes = jnp.einsum(
            "bij,bi->bj", jacobian, impulse_field, preferred_element_type=jnp.float32
        )
        pushes = jnp.transpose(pushes.reshape(blocks, 6, GB), (1, 0, 2))
        nearby = jnp.zeros((6, 9 * grains), jnp.float32).at[:, grain_slots].add(pushes)
        nearby = nearby.reshape(6, 3, 3, grains)
        row_sums = nearby[:, :, 1]
        for step_y in (-1, 1):
            row_sums = row_sums + from_behind(
                nearby[:, :, step_y + 1].astype(jnp.bfloat16), GY, step_y
            ).astype(jnp.float32)
        summed = row_sums[:, 1]
        for step_x in (-1, 1):
            summed = summed + from_behind(row_sums[:, step_x + 1], GX, step_x)
        return summed

    constraint_bias = velocity_bias + forward(free_velocity.astype(jnp.bfloat16))
    extrapolated = impulse_start * live_mask
    previous = extrapolated
    current = extrapolated
    weights = momentum_weights(ITERS)
    for iteration in range(ITERS):
        pushed = backward(extrapolated.astype(jnp.bfloat16))
        moved = inverse_mass * pushed
        totals = lax.psum(
            jnp.stack([jnp.sum(extrapolated * extrapolated), jnp.sum(pushed * moved)]), GX_GY
        )
        size_total, energy_total = (totals[0], totals[1])
        gradient = (forward(moved.astype(jnp.bfloat16)) + constraint_bias) * live_mask
        step_size = size_total / (energy_total + epsilon)
        current = project_cone(extrapolated - step_size * gradient, friction) * live_mask
        extrapolated = current + weights[iteration] * (current - previous)
        previous = current
    final_push = backward(current.astype(jnp.bfloat16))
    return (current, free_velocity + inverse_mass * final_push)


def solution(mesh):
    finer = Mesh(mesh.devices.reshape(4, 4, 4, 2), ("gx_0", "gx_1", "gy_0", "gy_1"))
    placed = (
        P(GX_GY, None, None),
        P(GX_GY, None),
        P(GX_GY),
        P(GX_GY, None),
        P(GX_GY, None),
        P(GX_GY, None),
        P(None, GX_GY),
        P(None, GX_GY),
    )
    return jax.shard_map(
        shards,
        mesh=finer,
        in_specs=placed,
        out_specs=(P(GX_GY, None), P(None, GX_GY)),
        check_vma=False,
    )
```

profile of v0, /device:TPU:34, one launch (start us, length us, event | category | flops | bytes accessed | tf_op | source)
XLA Modules:
  0.0 789.8 jit_solution(12597441963960114974)
XLA Ops:
  1.5 4.5 collective-permute-start.9
  11.1 9.1 %fusion = f32[128,384]{1,0:T(8,128)S(1)} fusion(bf16[128,192,384]{2,1,0:T(8,128)(2,1)} %param.10, f32[128,192]{1,0:T(8,128)S(1)} %copy.120), kind=kLoop, calls=%fused_computation.16 | loop fusion | flops 28262400 | bytes 19169280
  20.4 4.5 copy.112
  24.9 48.5 %scatter_custom_fusion = f32[6,18432]{0,1:T(8,128)} fusion(s32[8192]{0:T(1024)S(1)} %reshape.145, f32[8192,6]{1,0:T(8,128)} %bitcast.184, f32[]{:T(128)} %constant.14.clone.1), kind=kCustom, calls=%fused_computation.30 | custom fusion | flops 49152 | bytes 442880 | tf_op jit(solution)/shard_map/scatter-add | solution.py:92
  73.4 5.6 copy.50
  88.7 6.0 collective-permute-start.2
  100.2 24.8 %gather_fusion.1 = bf16[8192,6]{1,0:T(8,128)(2,1)S(1)} fusion(bf16[6,18432]{0,1:T(8,128)(2,1)} %bitcast.180, s32[8192]{0:T(1024)S(1)} %broadcast_clamp_fusion), kind=kCustom, calls=%fused_computation.1.clone | custom fusion | bytes 229376 | tf_op jit(solution)/shard_map/jit(_take)/gather | solution.py:83
  125.7 6.0 collective-permute-start.5
  137.3 65.9 %psum.21 = f32[2]{0:T(128)S(1)} all-reduce(f32[2]{0:T(128)S(1)} %pad_maximum_fusion.8), channel_id=1, replica_groups=mesh['gx_0'=4,'gx_1'=4,'gy_0'=4,'gy_1'=2] {'gx_0','gx_1','gy_0','gy_1'}, use_global_device_ids=true, to_apply=%region_3.4 | all-reduce | flops 2 | bytes 16 | tf_op jit(solution)/shard_map/psum | solution.py:112
  215.9 24.8 %gather_fusion = bf16[8192,6]{1,0:T(8,128)(2,1)S(1)} fusion(bf16[6,18432]{0,1:T(8,128)(2,1)} %bitcast.181, s32[8192]{0:T(1024)S(1)} %broadcast_clamp_fusion), kind=kCustom, calls=%fused_computation.clone | custom fusion | bytes 229376 | tf_op jit(solution)/shard_map/jit(_take)/gather | solution.py:83
  243.4 29.2 %fusion.5 = (f32[128,192]{1,0:T(8,128)S(1)}, f32[128,192]{1,0:T(8,128)S(1)}) fusion(f32[128,384]{1,0:T(8,128)S(1)} %copy.122, bf16[128,192,384]{2,1,0:T(8,128)(2,1)} %param.10, f32[128,384]{1,0:T(8,128)S(1)} %copy.121), kind=kLoop, calls=%fused_computation.21 | loop fusion | flops 47136768 | bytes 19464192
  273.6 9.1 %fusion.1 = f32[128,384]{1,0:T(8,128)S(1)} fusion(bf16[128,192,384]{2,1,0:T(8,128)(2,1)} %param.10, f32[128,192]{1,0:T(8,128)S(1)} %copy.123), kind=kLoop, calls=%fused_computation.17 | loop fusion | flops 28262400 | bytes 19169280
  282.9 4.5 copy.113
  287.4 48.5 %scatter_custom_fusion.1 = f32[6,18432]{0,1:T(8,128)} fusion(s32[8192]{0:T(1024)S(1)} %reshape.145, f32[8192,6]{1,0:T(8,128)} %bitcast.185, f32[]{:T(128)} %constant.14.clone.1), kind=kCustom, calls=%fused_computation.28 | custom fusion | flops 49152 | bytes 442880 | tf_op jit(solution)/shard_map/scatter-add | solution.py:92
  335.9 5.6 copy.60
  355.8 5.8 collective-permute-done.15
  369.4 61.6 %psum.22 = f32[2]{0:T(128)S(1)} all-reduce(f32[2]{0:T(128)S(1)} %pad_maximum_fusion.9), channel_id=1, replica_groups=mesh['gx_0'=4,'gx_1'=4,'gy_0'=4,'gy_1'=2] {'gx_0','gx_1','gy_0','gy_1'}, use_global_device_ids=true, to_apply=%region_7.9 | all-reduce | flops 2 | bytes 16 | tf_op jit(solution)/shard_map/psum | solution.py:112
  443.4 24.8 %gather_fusion.2 = bf16[8192,6]{1,0:T(8,128)(2,1)S(1)} fusion(bf16[6,18432]{0,1:T(8,128)(2,1)} %bitcast.182, s32[8192]{0:T(1024)S(1)} %broadcast_clamp_fusion), kind=kCustom, calls=%fused_computation.2.clone | custom fusion | bytes 229376 | tf_op jit(solution)/shard_map/jit(_take)/gather | solution.py:83
  470.7 15.7 %fusion.6 = f32[128,192]{1,0:T(8,128)S(1)} fusion(f32[128,384]{1,0:T(8,128)S(1)} %copy.124, bf16[128,192,384]{2,1,0:T(8,128)(2,1)} %param.10), kind=kLoop, calls=%fused_computation.22 | loop fusion | flops 28286976 | bytes 19169280
  487.3 9.1 %fusion.2 = f32[128,384]{1,0:T(8,128)S(1)} fusion(bf16[128,192,384]{2,1,0:T(8,128)(2,1)} %param.10, f32[128,192]{1,0:T(8,128)S(1)} %copy.125), kind=kLoop, calls=%fused_computation.18 | loop fusion | flops 28262400 | bytes 19169280
  496.6 4.5 copy.114
  501.1 48.5 %scatter_custom_fusion.2 = f32[6,18432]{0,1:T(8,128)} fusion(s32[8192]{0:T(1024)S(1)} %reshape.145, f32[8192,6]{1,0:T(8,128)} %bitcast.186, f32[]{:T(128)} %constant.14.clone.1), kind=kCustom, calls=%fused_computation.26 | custom fusion | flops 49152 | bytes 442880 | tf_op jit(solution)/shard_map/scatter-add | solution.py:92
  549.6 5.6 copy.67
  569.4 5.7 collective-permute-done.23
  582.9 61.4 %psum.23 = f32[2]{0:T(128)S(1)} all-reduce(f32[2]{0:T(128)S(1)} %pad_maximum_fusion.10), channel_id=1, replica_groups=mesh['gx_0'=4,'gx_1'=4,'gy_0'=4,'gy_1'=2] {'gx_0','gx_1','gy_0','gy_1'}, use_global_device_ids=true, to_apply=%region_11.13 | all-reduce | flops 2 | bytes 16 | tf_op jit(solution)/shard_map/psum | solution.py:112
  656.8 24.8 %gather_fusion.3 = bf16[8192,6]{1,0:T(8,128)(2,1)S(1)} fusion(bf16[6,18432]{0,1:T(8,128)(2,1)} %bitcast.179, s32[8192]{0:T(1024)S(1)} %broadcast_clamp_fusion), kind=kCustom, calls=%fused_computation.3.clone | custom fusion | bytes 229376 | tf_op jit(solution)/shard_map/jit(_take)/gather | solution.py:83
  684.1 15.7 %fusion.7 = f32[128,192]{1,0:T(8,128)S(1)} fusion(f32[128,384]{1,0:T(8,128)S(1)} %copy.126, bf16[128,192,384]{2,1,0:T(8,128)(2,1)} %param.10), kind=kLoop, calls=%fused_computation.23 | loop fusion | flops 28286976 | bytes 19169280
  700.7 9.1 %fusion.3 = f32[128,384]{1,0:T(8,128)S(1)} fusion(bf16[128,192,384]{2,1,0:T(8,128)(2,1)} %param.10, f32[128,192]{1,0:T(8,128)S(1)} %copy.127), kind=kLoop, calls=%fused_computation.19 | loop fusion | flops 28262400 | bytes 19169280
  710.0 4.5 copy.115
  714.5 48.5 %scatter_custom_fusion.3 = f32[6,18432]{0,1:T(8,128)} fusion(s32[8192]{0:T(1024)S(1)} %reshape.145, f32[8192,6]{1,0:T(8,128)} %bitcast.183, f32[]{:T(128)} %constant.14.clone.1), kind=kCustom, calls=%fused_computation.24 | custom fusion | flops 49152 | bytes 442880 | tf_op jit(solution)/shard_map/scatter-add | solution.py:92
  763.0 5.6 copy.74
  782.8 6.2 collective-permute-done.31
  (156 shorter events, 129.5 us)
Async XLA Ops:
  1.5 82.0 %collective-permute-start.9 = (bf16[6,1,1,2048]{3,0,2,1:T(8,128)(2,1)S(1)}, bf16[6,1,1,2048]{3,0,2,1:T(8,128)(2,1)S(1)}, u32[]{:S(2)}, u32[]{:S(2)}) collective-permute-start(bf16[6,1,1,2048]{3,0,2,1:T(8,128)(2,1)S(1)} %convert_bitcast_fusion), channel_id=1, source_target_pairs={{8,0},{16,8},{24,16},{32,24},{40,32},{48,40},{56,48},{64,56},{72,6... | collective-permute-start | bytes 73736 | tf_op jit(solution)/shard_map/ppermute | solution.py:25
  5.9 77.5 %collective-permute-start.8 = (bf16[6,1,1,2048]{3,0,2,1:T(8,128)(2,1)S(1)}, bf16[6,1,1,2048]{3,0,2,1:T(8,128)(2,1)S(1)}, u32[]{:S(2)}, u32[]{:S(2)}) collective-permute-start(bf16[6,1,1,2048]{3,0,2,1:T(8,128)(2,1)S(1)} %convert_bitcast_fusion), channel_id=1, source_target_pairs={{0,8},{8,16},{16,24},{24,32},{32,40},{40,48},{48,56},{56,64},{64,7... | collective-permute-start | bytes 73736 | tf_op jit(solution)/shard_map/ppermute | solution.py:24
  79.1 9.5 %collective-permute-start = (bf16[6,3,2048]{2,0,1:T(8,128)(2,1)S(1)}, bf16[6,3,2048]{2,0,1:T(8,128)(2,1)S(1)}, u32[]{:S(2)}, u32[]{:S(2)}) collective-permute-start(bf16[6,3,2048]{2,0,1:T(8,128)(2,1)S(1)} %get-tuple-element.31), channel_id=1, source_target_pairs={{1,0},{2,1},{3,2},{4,3},{5,4},{6,5},{7,6},{9,8},{10,9},{11,10},{12... | collective-permute-start | bytes 221192 | tf_op jit(solution)/shard_map/ppermute | solution.py:33
  81.0 7.6 collective-permute-start.1
  83.5 13.1 %collective-permute-start.11 = (bf16[6,3,1,2048]{3,0,2,1:T(8,128)(2,1)S(1)}, bf16[6,3,1,2048]{3,0,2,1:T(8,128)(2,1)S(1)}, u32[]{:S(2)}, u32[]{:S(2)}) collective-permute-start(bf16[6,3,1,2048]{3,0,2,1:T(8,128)(2,1)S(1)} %pad_maximum_fusion.5), channel_id=1, source_target_pairs={{1,0},{2,1},{3,2},{4,3},{5,4},{6,5},{7,6},{9,8},{10,9},{11,10},{12... | collective-permute-start | bytes 221192 | tf_op jit(solution)/shard_map/ppermute | solution.py:25
  86.7 10.0 %collective-permute-start.10 = (bf16[6,3,1,2048]{3,0,2,1:T(8,128)(2,1)S(1)}, bf16[6,3,1,2048]{3,0,2,1:T(8,128)(2,1)S(1)}, u32[]{:S(2)}, u32[]{:S(2)}) collective-permute-start(bf16[6,3,1,2048]{3,0,2,1:T(8,128)(2,1)S(1)} %pad_maximum_fusion.5), channel_id=1, source_target_pairs={{0,1},{1,2},{2,3},{3,4},{4,5},{5,6},{6,7},{8,9},{9,10},{10,11},{11... | collective-permute-start | bytes 221192 | tf_op jit(solution)/shard_map/ppermute | solution.py:24
  88.7 36.4 %collective-permute-start.2 = (f32[6,2048]{1,0:T(8,128)S(1)}, f32[6,2048]{1,0:T(8,128)S(1)}, u32[]{:S(2)}, u32[]{:S(2)}) collective-permute-start(f32[6,2048]{1,0:T(8,128)S(1)} %get-tuple-element.39), channel_id=1, source_target_pairs={{8,0},{16,8},{24,16},{32,24},{40,32},{48,40},{56,48},{64,56},{72,6... | collective-permute-start | bytes 147464 | tf_op jit(solution)/shard_map/ppermute | solution.py:33
  94.7 30.4 %collective-permute-start.3 = (f32[6,2048]{1,0:T(8,128)S(1)}, f32[6,2048]{1,0:T(8,128)S(1)}, u32[]{:S(2)}, u32[]{:S(2)}) collective-permute-start(f32[6,2048]{1,0:T(8,128)S(1)} %get-tuple-element.40), channel_id=1, source_target_pairs={{0,8},{8,16},{16,24},{24,32},{32,40},{40,48},{48,56},{56,64},{64,7... | collective-permute-start | bytes 147464 | tf_op jit(solution)/shard_map/ppermute | solution.py:33
  125.7 77.5 %collective-permute-start.5 = (bf16[6,1,1,2048]{3,0,2,1:T(8,128)(2,1)S(1)}, bf16[6,1,1,2048]{3,0,2,1:T(8,128)(2,1)S(1)}, u32[]{:S(2)}, u32[]{:S(2)}) collective-permute-start(bf16[6,1,1,2048]{3,0,2,1:T(8,128)(2,1)S(1)} %get-tuple-element.24), channel_id=1, source_target_pairs={{8,0},{16,8},{24,16},{32,24},{40,32},{48,40},{56,48},{64,56},{72,6... | collective-permute-start | bytes 73736 | tf_op jit(solution)/shard_map/ppermute | solution.py:25
  131.8 71.5 %collective-permute-start.4 = (bf16[6,1,1,2048]{3,0,2,1:T(8,128)(2,1)S(1)}, bf16[6,1,1,2048]{3,0,2,1:T(8,128)(2,1)S(1)}, u32[]{:S(2)}, u32[]{:S(2)}) collective-permute-start(bf16[6,1,1,2048]{3,0,2,1:T(8,128)(2,1)S(1)} %get-tuple-element.24), channel_id=1, source_target_pairs={{0,8},{8,16},{16,24},{24,32},{32,40},{40,48},{48,56},{56,64},{64,7... | collective-permute-start | bytes 73736 | tf_op jit(solution)/shard_map/ppermute | solution.py:24
  203.3 7.4 collective-permute-start.7
  206.4 5.9 collective-permute-start.6
  341.6 4.3 collective-permute-start.12
  343.6 5.9 collective-permute-start.13
  349.6 6.2 collective-permute-start.14
  353.3 8.3 %collective-permute-start.15 = (f32[6,2048]{1,0:T(8,128)S(1)}, f32[6,2048]{1,0:T(8,128)S(1)}, u32[]{:S(2)}, u32[]{:S(2)}) collective-permute-start(f32[6,2048]{1,0:T(8,128)S(1)} %get-tuple-element.38), channel_id=1, source_target_pairs={{0,8},{8,16},{16,24},{24,32},{32,40},{40,48},{48,56},{56,64},{64,7... | collective-permute-start | bytes 147464 | tf_op jit(solution)/shard_map/ppermute | solution.py:33
  362.2 68.8 %collective-permute-start.17 = (bf16[6,1,1,2048]{3,0,2,1:T(8,128)(2,1)S(1)}, bf16[6,1,1,2048]{3,0,2,1:T(8,128)(2,1)S(1)}, u32[]{:S(2)}, u32[]{:S(2)}) collective-permute-start(bf16[6,1,1,2048]{3,0,2,1:T(8,128)(2,1)S(1)} %get-tuple-element.22), channel_id=1, source_target_pairs={{8,0},{16,8},{24,16},{32,24},{40,32},{48,40},{56,48},{64,56},{72,6... | collective-permute-start | bytes 73736 | tf_op jit(solution)/shard_map/ppermute | solution.py:25
  364.1 66.9 %collective-permute-start.16 = (bf16[6,1,1,2048]{3,0,2,1:T(8,128)(2,1)S(1)}, bf16[6,1,1,2048]{3,0,2,1:T(8,128)(2,1)S(1)}, u32[]{:S(2)}, u32[]{:S(2)}) collective-permute-start(bf16[6,1,1,2048]{3,0,2,1:T(8,128)(2,1)S(1)} %get-tuple-element.22), channel_id=1, source_target_pairs={{0,8},{8,16},{16,24},{24,32},{32,40},{40,48},{48,56},{56,64},{64,7... | collective-permute-start | bytes 73736 | tf_op jit(solution)/shard_map/ppermute | solution.py:24
  431.0 6.8 collective-permute-start.19
  433.9 5.9 collective-permute-start.18
  555.3 4.3 collective-permute-start.20
  557.2 5.9 collective-permute-start.21
  563.2 6.2 collective-permute-start.22
  566.8 8.3 %collective-permute-start.23 = (f32[6,2048]{1,0:T(8,128)S(1)}, f32[6,2048]{1,0:T(8,128)S(1)}, u32[]{:S(2)}, u32[]{:S(2)}) collective-permute-start(f32[6,2048]{1,0:T(8,128)S(1)} %get-tuple-element.36), channel_id=1, source_target_pairs={{0,8},{8,16},{16,24},{24,32},{32,40},{40,48},{48,56},{56,64},{64,7... | collective-permute-start | bytes 147464 | tf_op jit(solution)/shard_map/ppermute | solution.py:33
  575.7 68.6 %collective-permute-start.25 = (bf16[6,1,1,2048]{3,0,2,1:T(8,128)(2,1)S(1)}, bf16[6,1,1,2048]{3,0,2,1:T(8,128)(2,1)S(1)}, u32[]{:S(2)}, u32[]{:S(2)}) collective-permute-start(bf16[6,1,1,2048]{3,0,2,1:T(8,128)(2,1)S(1)} %get-tuple-element.20), channel_id=1, source_target_pairs={{8,0},{16,8},{24,16},{32,24},{40,32},{48,40},{56,48},{64,56},{72,6... | collective-permute-start | bytes 73736 | tf_op jit(solution)/shard_map/ppermute | solution.py:25
  577.6 66.7 %collective-permute-start.24 = (bf16[6,1,1,2048]{3,0,2,1:T(8,128)(2,1)S(1)}, bf16[6,1,1,2048]{3,0,2,1:T(8,128)(2,1)S(1)}, u32[]{:S(2)}, u32[]{:S(2)}) collective-permute-start(bf16[6,1,1,2048]{3,0,2,1:T(8,128)(2,1)S(1)} %get-tuple-element.20), channel_id=1, source_target_pairs={{0,8},{8,16},{16,24},{24,32},{32,40},{40,48},{48,56},{56,64},{64,7... | collective-permute-start | bytes 73736 | tf_op jit(solution)/shard_map/ppermute | solution.py:24
  644.4 6.8 collective-permute-start.27
  647.3 5.9 collective-permute-start.26
  768.7 4.3 collective-permute-start.28
  770.6 5.9 collective-permute-start.29
  776.6 6.2 collective-permute-start.30
  780.7 8.3 %collective-permute-start.31 = (f32[6,2048]{1,0:T(8,128)S(1)}, f32[6,2048]{1,0:T(8,128)S(1)}, u32[]{:S(2)}, u32[]{:S(2)}) collective-permute-start(f32[6,2048]{1,0:T(8,128)S(1)} %get-tuple-element.34), channel_id=1, source_target_pairs={{0,8},{8,16},{16,24},{24,32},{32,40},{40,48},{48,56},{56,64},{64,7... | collective-permute-start | bytes 147464 | tf_op jit(solution)/shard_map/ppermute | solution.py:33
  (6 other events, 273.1 us)
where the time goes:
time: 799 us; the launch traced here: 790 us
  other arithmetic  304 us (38%)
  blocking collectives  189 us (24%)
  local copies, waits for them, and re-layouts  167 us (21%)
  starting transfers between devices  89.1 us (11%)
  waiting for transfers between devices  35 us (4%)
    scatter-add x4, other arithmetic, backward(): jnp.zeros((6, 9 * grains), jnp.float32).at[:, grain_slots].add(pushes)  194 us
    psum x3, blocking collectives, shards(): lax.psum(jnp.stack([jnp.sum(extrapolated * extrapolated), jnp.sum(pushed...  189 us
    gather x8, local copies, waits for them, and re-layouts, forward(): picked = jnp.take(nearby, grain_slots, axis=1)  108 us
    unnamed x13, other arithmetic  97.8 us
    ppermute x16, starting transfers between devices, from_behind(): return lax.ppermute(block, axis, route)  42.9 us
    ppermute x16, waiting for transfers between devices, from_behind(): return lax.ppermute(block, axis, route)  29.1 us
    ppermute x8, starting transfers between devices, with_halo(): after = lax.ppermute(leading, axis, down)  26.4 us
    reshape x4, local copies, waits for them, and re-layouts, backward(): nearby = nearby.reshape(6, 3, 3, grains)  22.5 us
  transfers between devices with their start and end apart: 32, of which 12 were waited for; matrix products, arithmetic and copies ran while one was open for 14% of the time, Pallas kernels for 0%

commit v1 on v0

--- a/solution.py
+++ b/solution.py
@@ -109,9 +109,10 @@
     for iteration in range(ITERS):
         pushed = backward(extrapolated.astype(jnp.bfloat16))
         moved = inverse_mass * pushed
-        totals = lax.psum(
-            jnp.stack([jnp.sum(extrapolated * extrapolated), jnp.sum(pushed * moved)]), GX_GY
-        )
+        totals = lax.all_gather(
+            jnp.stack([jnp.sum(extrapolated * extrapolated), jnp.sum(pushed * moved)]),
+            axis_name=GX_GY,
+        ).sum(axis=0)
         size_total, energy_total = (totals[0], totals[1])
         gradient = (forward(moved.astype(jnp.bfloat16)) + constraint_bias) * live_mask
         step_size = size_total / (energy_total + epsilon)

time: 799 us -> 805 us (level)
  starting transfers between devices: 89.1 us -> 101 us
    psum x3 -> x0, blocking collectives: 189 us -> none  [shards(): lax.psum(jnp.stack([jnp.sum(extrapolated * extrapolated), jnp.sum(pushed...]
    unnamed x0 -> x3, blocking collectives: none -> 186 us
    ppermute x8, starting transfers between devices: 26.4 us -> 36.5 us  [with_halo(): after = lax.ppermute(leading, axis, down)]
    unnamed x13 -> x16, other arithmetic: 97.8 us -> 102 us
  transfers between devices with their start and end apart: 32 -> 32, of which waited for: 12 -> 11; matrix products, arithmetic and copies ran while one was open for 14% -> 13% of each run, Pallas kernels for 0% -> 0%
where the time goes in v1:
time: 805 us; the launch traced here: 796 us
  other arithmetic  304 us (38%)
  blocking collectives  186 us (23%)
  local copies, waits for them, and re-layouts  167 us (21%)
  starting transfers between devices  101 us (13%)
  waiting for transfers between devices  31.7 us (4%)
    scatter-add x4, other arithmetic, backward(): jnp.zeros((6, 9 * grains), jnp.float32).at[:, grain_slots].add(pushes)  194 us
    unnamed x3, blocking collectives  186 us
    gather x8, local copies, waits for them, and re-layouts, forward(): picked = jnp.take(nearby, grain_slots, axis=1)  108 us
    unnamed x16, other arithmetic  102 us
    ppermute x16, starting transfers between devices, from_behind(): return lax.ppermute(block, axis, route)  46.4 us
    ppermute x8, starting transfers between devices, with_halo(): after = lax.ppermute(leading, axis, down)  36.5 us
    ppermute x16, waiting for transfers between devices, from_behind(): return lax.ppermute(block, axis, route)  31 us
    reshape x4, local copies, waits for them, and re-layouts, backward(): nearby = nearby.reshape(6, 3, 3, grains)  22.5 us
  transfers between devices with their start and end apart: 32, of which 11 were waited for; matrix products, arithmetic and copies ran while one was open for 13% of the time, Pallas kernels for 0%

profile of v1, /device:TPU:34, one launch (start us, length us, event | category | flops | bytes accessed | tf_op | source)
XLA Modules:
  0.0 795.5 jit_solution(5879586189488415738)
XLA Ops:
  11.7 9.1 %fusion = f32[128,384]{1,0:T(8,128)S(1)} fusion(bf16[128,192,384]{2,1,0:T(8,128)(2,1)} %param.10, f32[128,192]{1,0:T(8,128)S(1)} %copy.120), kind=kLoop, calls=%fused_computation.16 | loop fusion | flops 28262400 | bytes 19169280
  25.7 48.5 %scatter_custom_fusion = f32[6,18432]{0,1:T(8,128)} fusion(s32[8192]{0:T(1024)S(1)} %reshape.145, f32[8192,6]{1,0:T(8,128)} %bitcast.183, f32[]{:T(128)} %constant.14.clone.1), kind=kCustom, calls=%fused_computation.30 | custom fusion | flops 49152 | bytes 442880 | tf_op jit(solution)/shard_map/scatter-add | solution.py:92
  74.2 5.6 copy.50
  99.4 24.8 %gather_fusion.1 = bf16[8192,6]{1,0:T(8,128)(2,1)S(1)} fusion(bf16[6,18432]{0,1:T(8,128)(2,1)} %bitcast.180, s32[8192]{0:T(1024)S(1)} %broadcast_clamp_fusion), kind=kCustom, calls=%fused_computation.1.clone | custom fusion | bytes 229376 | tf_op jit(solution)/shard_map/jit(_take)/gather | solution.py:83
  129.1 6.0 collective-permute-start.5
  136.6 63.2 %all-reduce = f32[256]{0:T(256)S(1)} all-reduce(f32[256]{0:T(256)S(1)} %maximum_dynamic-update-slice_fusion), channel_id=2, replica_groups=mesh['gx_0'=4,'gx_1'=4,'gy_0'=4,'gy_1'=2] {'gx_0','gx_1','gy_0','gy_1'}, use_global_device_ids=true, to_apply=%add | all-reduce | flops 256 | bytes 2048
  211.6 24.8 %gather_fusion = bf16[8192,6]{1,0:T(8,128)(2,1)S(1)} fusion(bf16[6,18432]{0,1:T(8,128)(2,1)} %bitcast.181, s32[8192]{0:T(1024)S(1)} %broadcast_clamp_fusion), kind=kCustom, calls=%fused_computation.clone | custom fusion | bytes 229376 | tf_op jit(solution)/shard_map/jit(_take)/gather | solution.py:83
  239.1 29.2 %fusion.5 = (f32[128,192]{1,0:T(8,128)S(1)}, f32[128,192]{1,0:T(8,128)S(1)}) fusion(f32[128,384]{1,0:T(8,128)S(1)} %copy.122, bf16[128,192,384]{2,1,0:T(8,128)(2,1)} %param.10, f32[128,384]{1,0:T(8,128)S(1)} %copy.121), kind=kLoop, calls=%fused_computation.21 | loop fusion | flops 47136768 | bytes 19464192
  269.3 9.1 %fusion.1 = f32[128,384]{1,0:T(8,128)S(1)} fusion(bf16[128,192,384]{2,1,0:T(8,128)(2,1)} %param.10, f32[128,192]{1,0:T(8,128)S(1)} %copy.123), kind=kLoop, calls=%fused_computation.17 | loop fusion | flops 28262400 | bytes 19169280
  278.6 4.5 copy.113
  283.1 48.5 %scatter_custom_fusion.1 = f32[6,18432]{0,1:T(8,128)} fusion(s32[8192]{0:T(1024)S(1)} %reshape.145, f32[8192,6]{1,0:T(8,128)} %bitcast.185, f32[]{:T(128)} %constant.14.clone.1), kind=kCustom, calls=%fused_computation.28 | custom fusion | flops 49152 | bytes 442880 | tf_op jit(solution)/shard_map/scatter-add | solution.py:92
  331.6 5.6 copy.60
  346.8 5.0 collective-permute-start.14
  353.8 6.3 collective-permute-done.15
  362.7 6.0 collective-permute-start.17
  370.4 61.3 %all-reduce.1 = f32[256]{0:T(256)S(1)} all-reduce(f32[256]{0:T(256)S(1)} %maximum_dynamic-update-slice_fusion.1), channel_id=3, replica_groups=mesh['gx_0'=4,'gx_1'=4,'gy_0'=4,'gy_1'=2] {'gx_0','gx_1','gy_0','gy_1'}, use_global_device_ids=true, to_apply=%add.1 | all-reduce | flops 256 | bytes 2048
  443.2 24.8 %gather_fusion.2 = bf16[8192,6]{1,0:T(8,128)(2,1)S(1)} fusion(bf16[6,18432]{0,1:T(8,128)(2,1)} %bitcast.182, s32[8192]{0:T(1024)S(1)} %broadcast_clamp_fusion), kind=kCustom, calls=%fused_computation.2.clone | custom fusion | bytes 229376 | tf_op jit(solution)/shard_map/jit(_take)/gather | solution.py:83
  470.5 15.7 %fusion.6 = f32[128,192]{1,0:T(8,128)S(1)} fusion(f32[128,384]{1,0:T(8,128)S(1)} %copy.124, bf16[128,192,384]{2,1,0:T(8,128)(2,1)} %param.10), kind=kLoop, calls=%fused_computation.22 | loop fusion | flops 28286976 | bytes 19169280
  487.1 9.1 %fusion.2 = f32[128,384]{1,0:T(8,128)S(1)} fusion(bf16[128,192,384]{2,1,0:T(8,128)(2,1)} %param.10, f32[128,192]{1,0:T(8,128)S(1)} %copy.125), kind=kLoop, calls=%fused_computation.18 | loop fusion | flops 28262400 | bytes 19169280
  496.4 4.5 copy.114
  500.9 48.5 %scatter_custom_fusion.2 = f32[6,18432]{0,1:T(8,128)} fusion(s32[8192]{0:T(1024)S(1)} %reshape.145, f32[8192,6]{1,0:T(8,128)} %bitcast.186, f32[]{:T(128)} %constant.14.clone.1), kind=kCustom, calls=%fused_computation.26 | custom fusion | flops 49152 | bytes 442880 | tf_op jit(solution)/shard_map/scatter-add | solution.py:92
  549.4 5.6 copy.67
  571.2 6.3 collective-permute-done.23
  580.1 6.0 collective-permute-start.25
  587.6 61.4 %all-reduce.2 = f32[256]{0:T(256)S(1)} all-reduce(f32[256]{0:T(256)S(1)} %maximum_dynamic-update-slice_fusion.2), channel_id=4, replica_groups=mesh['gx_0'=4,'gx_1'=4,'gy_0'=4,'gy_1'=2] {'gx_0','gx_1','gy_0','gy_1'}, use_global_device_ids=true, to_apply=%add.2 | all-reduce | flops 256 | bytes 2048
  660.5 24.8 %gather_fusion.3 = bf16[8192,6]{1,0:T(8,128)(2,1)S(1)} fusion(bf16[6,18432]{0,1:T(8,128)(2,1)} %bitcast.179, s32[8192]{0:T(1024)S(1)} %broadcast_clamp_fusion), kind=kCustom, calls=%fused_computation.3.clone | custom fusion | bytes 229376 | tf_op jit(solution)/shard_map/jit(_take)/gather | solution.py:83
  687.8 15.7 %fusion.7 = f32[128,192]{1,0:T(8,128)S(1)} fusion(f32[128,384]{1,0:T(8,128)S(1)} %copy.126, bf16[128,192,384]{2,1,0:T(8,128)(2,1)} %param.10), kind=kLoop, calls=%fused_computation.23 | loop fusion | flops 28286976 | bytes 19169280
  704.5 9.1 %fusion.3 = f32[128,384]{1,0:T(8,128)S(1)} fusion(bf16[128,192,384]{2,1,0:T(8,128)(2,1)} %param.10, f32[128,192]{1,0:T(8,128)S(1)} %copy.127), kind=kLoop, calls=%fused_computation.19 | loop fusion | flops 28262400 | bytes 19169280
  713.7 4.5 copy.115
  718.2 48.5 %scatter_custom_fusion.3 = f32[6,18432]{0,1:T(8,128)} fusion(s32[8192]{0:T(1024)S(1)} %reshape.145, f32[8192,6]{1,0:T(8,128)} %bitcast.184, f32[]{:T(128)} %constant.14.clone.1), kind=kCustom, calls=%fused_computation.24 | custom fusion | flops 49152 | bytes 442880 | tf_op jit(solution)/shard_map/scatter-add | solution.py:92
  766.7 5.6 copy.74
  788.3 6.3 collective-permute-done.31
  (165 shorter events, 134.7 us)
Async XLA Ops:
  1.5 82.8 %collective-permute-start.8 = (bf16[6,1,1,2048]{3,0,2,1:T(8,128)(2,1)S(1)}, bf16[6,1,1,2048]{3,0,2,1:T(8,128)(2,1)S(1)}, u32[]{:S(2)}, u32[]{:S(2)}) collective-permute-start(bf16[6,1,1,2048]{3,0,2,1:T(8,128)(2,1)S(1)} %convert_bitcast_fusion), channel_id=1, source_target_pairs={{0,8},{8,16},{16,24},{24,32},{32,40},{40,48},{48,56},{56,64},{64,7... | collective-permute-start | bytes 73736 | tf_op jit(solution)/shard_map/ppermute | solution.py:24
  5.0 79.3 %collective-permute-start.9 = (bf16[6,1,1,2048]{3,0,2,1:T(8,128)(2,1)S(1)}, bf16[6,1,1,2048]{3,0,2,1:T(8,128)(2,1)S(1)}, u32[]{:S(2)}, u32[]{:S(2)}) collective-permute-start(bf16[6,1,1,2048]{3,0,2,1:T(8,128)(2,1)S(1)} %convert_bitcast_fusion), channel_id=1, source_target_pairs={{8,0},{16,8},{24,16},{32,24},{40,32},{48,40},{56,48},{64,56},{72,6... | collective-permute-start | bytes 73736 | tf_op jit(solution)/shard_map/ppermute | solution.py:25
  79.9 10.0 %collective-permute-start = (bf16[6,3,2048]{2,0,1:T(8,128)(2,1)S(1)}, bf16[6,3,2048]{2,0,1:T(8,128)(2,1)S(1)}, u32[]{:S(2)}, u32[]{:S(2)}) collective-permute-start(bf16[6,3,2048]{2,0,1:T(8,128)(2,1)S(1)} %get-tuple-element.31), channel_id=1, source_target_pairs={{1,0},{2,1},{3,2},{4,3},{5,4},{6,5},{7,6},{9,8},{10,9},{11,10},{12... | collective-permute-start | bytes 221192 | tf_op jit(solution)/shard_map/ppermute | solution.py:33
  81.8 8.1 %collective-permute-start.1 = (bf16[6,3,2048]{2,0,1:T(8,128)(2,1)S(1)}, bf16[6,3,2048]{2,0,1:T(8,128)(2,1)S(1)}, u32[]{:S(2)}, u32[]{:S(2)}) collective-permute-start(bf16[6,3,2048]{2,0,1:T(8,128)(2,1)S(1)} %get-tuple-element.32), channel_id=1, source_target_pairs={{0,1},{1,2},{2,3},{3,4},{4,5},{5,6},{6,7},{8,9},{9,10},{10,11},{11... | collective-permute-start | bytes 221192 | tf_op jit(solution)/shard_map/ppermute | solution.py:33
  84.3 11.5 %collective-permute-start.10 = (bf16[6,3,1,2048]{3,0,2,1:T(8,128)(2,1)S(1)}, bf16[6,3,1,2048]{3,0,2,1:T(8,128)(2,1)S(1)}, u32[]{:S(2)}, u32[]{:S(2)}) collective-permute-start(bf16[6,3,1,2048]{3,0,2,1:T(8,128)(2,1)S(1)} %pad_maximum_fusion.5), channel_id=1, source_target_pairs={{0,1},{1,2},{2,3},{3,4},{4,5},{5,6},{6,7},{8,9},{9,10},{10,11},{11... | collective-permute-start | bytes 221192 | tf_op jit(solution)/shard_map/ppermute | solution.py:24
  87.4 8.5 %collective-permute-start.11 = (bf16[6,3,1,2048]{3,0,2,1:T(8,128)(2,1)S(1)}, bf16[6,3,1,2048]{3,0,2,1:T(8,128)(2,1)S(1)}, u32[]{:S(2)}, u32[]{:S(2)}) collective-permute-start(bf16[6,3,1,2048]{3,0,2,1:T(8,128)(2,1)S(1)} %pad_maximum_fusion.5), channel_id=1, source_target_pairs={{1,0},{2,1},{3,2},{4,3},{5,4},{6,5},{7,6},{9,8},{10,9},{11,10},{12... | collective-permute-start | bytes 221192 | tf_op jit(solution)/shard_map/ppermute | solution.py:25
  90.0 36.5 %collective-permute-start.2 = (f32[6,2048]{1,0:T(8,128)S(1)}, f32[6,2048]{1,0:T(8,128)S(1)}, u32[]{:S(2)}, u32[]{:S(2)}) collective-permute-start(f32[6,2048]{1,0:T(8,128)S(1)} %get-tuple-element.39), channel_id=1, source_target_pairs={{8,0},{16,8},{24,16},{32,24},{40,32},{48,40},{56,48},{64,56},{72,6... | collective-permute-start | bytes 147464 | tf_op jit(solution)/shard_map/ppermute | solution.py:33
  92.4 34.2 %collective-permute-start.3 = (f32[6,2048]{1,0:T(8,128)S(1)}, f32[6,2048]{1,0:T(8,128)S(1)}, u32[]{:S(2)}, u32[]{:S(2)}) collective-permute-start(f32[6,2048]{1,0:T(8,128)S(1)} %get-tuple-element.40), channel_id=1, source_target_pairs={{0,8},{8,16},{16,24},{24,32},{32,40},{40,48},{48,56},{56,64},{64,7... | collective-permute-start | bytes 147464 | tf_op jit(solution)/shard_map/ppermute | solution.py:33
  127.2 72.8 %collective-permute-start.4 = (bf16[6,1,1,2048]{3,0,2,1:T(8,128)(2,1)S(1)}, bf16[6,1,1,2048]{3,0,2,1:T(8,128)(2,1)S(1)}, u32[]{:S(2)}, u32[]{:S(2)}) collective-permute-start(bf16[6,1,1,2048]{3,0,2,1:T(8,128)(2,1)S(1)} %get-tuple-element.24), channel_id=1, source_target_pairs={{0,8},{8,16},{16,24},{24,32},{32,40},{40,48},{48,56},{56,64},{64,7... | collective-permute-start | bytes 73736 | tf_op jit(solution)/shard_map/ppermute | solution.py:24
  129.1 70.9 %collective-permute-start.5 = (bf16[6,1,1,2048]{3,0,2,1:T(8,128)(2,1)S(1)}, bf16[6,1,1,2048]{3,0,2,1:T(8,128)(2,1)S(1)}, u32[]{:S(2)}, u32[]{:S(2)}) collective-permute-start(bf16[6,1,1,2048]{3,0,2,1:T(8,128)(2,1)S(1)} %get-tuple-element.24), channel_id=1, source_target_pairs={{8,0},{16,8},{24,16},{32,24},{40,32},{48,40},{56,48},{64,56},{72,6... | collective-permute-start | bytes 73736 | tf_op jit(solution)/shard_map/ppermute | solution.py:25
  200.1 7.9 collective-permute-start.6
  202.0 6.0 collective-permute-start.7
  337.3 5.7 collective-permute-start.12
  340.9 5.9 collective-permute-start.13
  346.8 7.0 collective-permute-start.14
  351.9 8.3 %collective-permute-start.15 = (f32[6,2048]{1,0:T(8,128)S(1)}, f32[6,2048]{1,0:T(8,128)S(1)}, u32[]{:S(2)}, u32[]{:S(2)}) collective-permute-start(f32[6,2048]{1,0:T(8,128)S(1)} %get-tuple-element.38), channel_id=1, source_target_pairs={{0,8},{8,16},{16,24},{24,32},{32,40},{40,48},{48,56},{56,64},{64,7... | collective-permute-start | bytes 147464 | tf_op jit(solution)/shard_map/ppermute | solution.py:33
  360.8 71.0 %collective-permute-start.16 = (bf16[6,1,1,2048]{3,0,2,1:T(8,128)(2,1)S(1)}, bf16[6,1,1,2048]{3,0,2,1:T(8,128)(2,1)S(1)}, u32[]{:S(2)}, u32[]{:S(2)}) collective-permute-start(bf16[6,1,1,2048]{3,0,2,1:T(8,128)(2,1)S(1)} %get-tuple-element.22), channel_id=1, source_target_pairs={{0,8},{8,16},{16,24},{24,32},{32,40},{40,48},{48,56},{56,64},{64,7... | collective-permute-start | bytes 73736 | tf_op jit(solution)/shard_map/ppermute | solution.py:24
  362.7 69.1 %collective-permute-start.17 = (bf16[6,1,1,2048]{3,0,2,1:T(8,128)(2,1)S(1)}, bf16[6,1,1,2048]{3,0,2,1:T(8,128)(2,1)S(1)}, u32[]{:S(2)}, u32[]{:S(2)}) collective-permute-start(bf16[6,1,1,2048]{3,0,2,1:T(8,128)(2,1)S(1)} %get-tuple-element.22), channel_id=1, source_target_pairs={{8,0},{16,8},{24,16},{32,24},{40,32},{48,40},{56,48},{64,56},{72,6... | collective-permute-start | bytes 73736 | tf_op jit(solution)/shard_map/ppermute | solution.py:25
  431.9 7.5 collective-permute-start.18
  433.8 5.8 collective-permute-start.19
  555.1 5.9 collective-permute-start.20
  558.8 5.9 collective-permute-start.21
  564.8 6.4 collective-permute-start.22
  569.3 8.3 %collective-permute-start.23 = (f32[6,2048]{1,0:T(8,128)S(1)}, f32[6,2048]{1,0:T(8,128)S(1)}, u32[]{:S(2)}, u32[]{:S(2)}) collective-permute-start(f32[6,2048]{1,0:T(8,128)S(1)} %get-tuple-element.36), channel_id=1, source_target_pairs={{0,8},{8,16},{16,24},{24,32},{32,40},{40,48},{48,56},{56,64},{64,7... | collective-permute-start | bytes 147464 | tf_op jit(solution)/shard_map/ppermute | solution.py:33
  578.2 71.0 %collective-permute-start.24 = (bf16[6,1,1,2048]{3,0,2,1:T(8,128)(2,1)S(1)}, bf16[6,1,1,2048]{3,0,2,1:T(8,128)(2,1)S(1)}, u32[]{:S(2)}, u32[]{:S(2)}) collective-permute-start(bf16[6,1,1,2048]{3,0,2,1:T(8,128)(2,1)S(1)} %get-tuple-element.20), channel_id=1, source_target_pairs={{0,8},{8,16},{16,24},{24,32},{32,40},{40,48},{48,56},{56,64},{64,7... | collective-permute-start | bytes 73736 | tf_op jit(solution)/shard_map/ppermute | solution.py:24
  580.1 69.1 %collective-permute-start.25 = (bf16[6,1,1,2048]{3,0,2,1:T(8,128)(2,1)S(1)}, bf16[6,1,1,2048]{3,0,2,1:T(8,128)(2,1)S(1)}, u32[]{:S(2)}, u32[]{:S(2)}) collective-permute-start(bf16[6,1,1,2048]{3,0,2,1:T(8,128)(2,1)S(1)} %get-tuple-element.20), channel_id=1, source_target_pairs={{8,0},{16,8},{24,16},{32,24},{40,32},{48,40},{56,48},{64,56},{72,6... | collective-permute-start | bytes 73736 | tf_op jit(solution)/shard_map/ppermute | solution.py:25
  649.2 7.5 collective-permute-start.26
  651.2 5.8 collective-permute-start.27
  772.4 5.9 collective-permute-start.28
  776.2 5.9 collective-permute-start.29
  782.2 6.2 collective-permute-start.30
  786.4 8.3 %collective-permute-start.31 = (f32[6,2048]{1,0:T(8,128)S(1)}, f32[6,2048]{1,0:T(8,128)S(1)}, u32[]{:S(2)}, u32[]{:S(2)}) collective-permute-start(f32[6,2048]{1,0:T(8,128)S(1)} %get-tuple-element.34), channel_id=1, source_target_pairs={{0,8},{8,16},{16,24},{24,32},{32,40},{40,48},{48,56},{56,64},{64,7... | collective-permute-start | bytes 147464 | tf_op jit(solution)/shard_map/ppermute | solution.py:33
  (6 other events, 230.9 us)
